TPU v7x, 256 devices: a whole 4x4x8 slice. The times are simulated.
256 devices in a mesh: axial: 16 (over z, core), circ: 16 (over x, y).
Axes of the slice: x: 4, y: 4, z: 8, core: 2. Of those that a mesh axis runs over, the one named last changes fastest.
Arguments:
- right_side: float32 [128, 256, 256], P('axial', 'circ'), may hold values from -6 to 6
- stiffness: float32 [128, 256, 256], P('axial', 'circ'), may hold values from 0.03 to 0.3
- material: int32 [128, 256, 256], P('axial', 'circ'), may hold values from 0 to 15
- groups: int32 [128, 256, 256], P('axial', 'circ'), may hold values from 0 to 7, as said below
Outputs:
- solution: float32 [128, 256, 256], P('axial', 'circ')
- residual: float32 [128, 256, 256], P('axial', 'circ')
Inputs may be any that keep to these rules, and one draw needn't show every extreme that they name: `groups`: in every column of cells along the third dimension every group number from 0 to 7 occurs.
All inputs are finite; a program needn't handle non-finite values.
Results may differ from a plain program's by a relative error of at most 0.0003.
Values sent between devices are 32-bit elements; how exact they have to be, the bound alone decides.
No kernel may reach another device: no remote copies, remote signals or barrier semaphores. Data moves between devices by JAX's collectives and lax.ppermute only.
A program may use at most 128 MiB of HBM per device.

v0:
```python
import functools
import math
import jax
import jax.numpy as jnp
import numpy as np
from jax import lax
from jax.sharding import Mesh
from jax.sharding import PartitionSpec as P

LABELS = 8
CLASSES = 16
ITERS = 2
CIRC = ("circ_0", "circ_1")
AXIAL = ("axial_0", "axial_1")
AXIAL_CIRC = ("axial_0", "axial_1", "circ_0", "circ_1")
MASS_SHIFT = 0.02
PRECISE = lax.Precision.HIGHEST
HALF_STEPS = (
    (0, 0, 1),
    (0, 1, -1),
    (0, 1, 0),
    (0, 1, 1),
    (1, -1, -1),
    (1, -1, 0),
    (1, -1, 1),
    (1, 0, -1),
    (1, 0, 0),
    (1, 0, 1),
    (1, 1, -1),
    (1, 1, 0),
    (1, 1, 1),
)


def with_halo(array, sides, width, wrap):
    for axis, dim in sides:
        peers, length = (lax.axis_size(axis), array.shape[dim])
        up = [(i, (i + 1) % peers) for i in range(peers if wrap else peers - 1)]
        down = [(j, i) for i, j in up]
        last = lax.slice_in_dim(array, length - width, length, axis=dim)
        first = lax.slice_in_dim(array, 0, width, axis=dim)
        before = lax.ppermute(last, axis, up)
        after = lax.ppermute(first, axis, down)
        array = jnp.concatenate([before, array, after], axis=dim)
    return array


def copy_for_each(array, axis):
    copies = jnp.broadcast_to(array, (lax.axis_size(axis), *array.shape))
    return lax.all_to_all(copies, axis, split_axis=0, concat_axis=0, tiled=True)


def in_order(parts, dim):
    shape = list(parts.shape[1:])
    shape[dim] *= parts.shape[0]
    return jnp.moveaxis(parts, 0, dim).reshape(shape)


def collect(array, axis, dim):
    parts = copy_for_each(array, axis)
    return in_order(parts, dim)


def gather_in_order(array, axes, turns):
    parts = array[None]
    for k in turns:
        parts = lax.all_gather(parts, axes[k], axis=0, tiled=True)
    held = [lax.axis_size(axes[k]) for k in reversed(turns)]
    parts = parts.reshape(*held, *array.shape)
    turned = sorted(range(len(turns)), key=lambda place: turns[len(turns) - 1 - place])
    return parts.transpose(*turned, *range(len(turns), parts.ndim)).reshape(-1, *array.shape)


def gather_axes(array, axes, turns, dim):
    return in_order(gather_in_order(array, axes, turns), dim)


def over_axes(array, axes):
    return functools.reduce(lax.psum, axes, array)


def coefficient_table():
    rows_out = []
    for material_id in range(CLASSES):
        fiber_angle = math.pi * (material_id % 8) / 8.0
        if material_id < 8:
            fiber_dir = (math.cos(fiber_angle), math.sin(fiber_angle), 0.0)
            strength, anisotropy = (1.0, 6.0)
        else:
            fiber_dir = (0.6 * math.cos(fiber_angle), 0.6 * math.sin(fiber_angle), 0.8)
            strength, anisotropy = (0.35, 2.0)
        line_values = []
        for offset in HALF_STEPS:
            length_sq = float(offset[0] * offset[0] + offset[1] * offset[1] + offset[2] * offset[2])
            along_fiber = (
                fiber_dir[0] * offset[0] + fiber_dir[1] * offset[1] + fiber_dir[2] * offset[2]
            )
            line_values.append(
                strength * (0.15 + anisotropy * along_fiber * along_fiber / length_sq) / length_sq
            )
        rows_out.append(line_values)
    return np.array(rows_out, dtype=np.float32)


def shift_radial(values_in, amount):
    if amount == 0:
        return values_in
    blank_edge = jnp.zeros(values_in.shape[:-1] + (1,), values_in.dtype)
    if amount > 0:
        return jnp.concatenate([values_in[..., 1:], blank_edge], axis=-1)
    return jnp.concatenate([blank_edge, values_in[..., :-1]], axis=-1)


def neighbour(padded, move_axial, move_circ, move_radial):
    rows_axial = padded.shape[-3] - 2
    rows_circ = padded.shape[-2] - 2
    window = padded[
        ...,
        1 + move_axial : 1 + move_axial + rows_axial,
        1 + move_circ : 1 + move_circ + rows_circ,
        :,
    ]
    return shift_radial(window, move_radial)


def extend_field(field):
    widened = with_halo(field, ((CIRC, 1),), 1, True)
    return with_halo(widened, ((AXIAL, 0),), 1, False)


def extend_labels(labels):
    widened = with_halo(labels, ((CIRC, 2),), 1, True)
    return with_halo(widened, ((AXIAL, 1),), 1, False)


def class_onehot(labels, class_count):
    levels = jnp.arange(class_count, dtype=jnp.int32).reshape((class_count,) + (1,) * labels.ndim)
    return (labels[None] == levels).astype(jnp.float32)


def edge_weights(stiff_pad, class_pad):
    looked_up = jnp.einsum(
        "mxyr,mj->jxyr",
        class_onehot(class_pad, CLASSES),
        jnp.asarray(coefficient_table()),
        precision=PRECISE,
    )
    coefficient = stiff_pad[None] * looked_up
    weights = []
    diagonal = None
    for position, offset in enumerate(HALF_STEPS):
        centre = coefficient[position, 1:-1, 1:-1]
        forward_weight = 0.5 * (
            centre + neighbour(coefficient[position], offset[0], offset[1], offset[2])
        )
        backward_weight = 0.5 * (
            centre + neighbour(coefficient[position], -offset[0], -offset[1], -offset[2])
        )
        weights.append((forward_weight, backward_weight))
        pair_sum = forward_weight + backward_weight
        diagonal = pair_sum if diagonal is None else diagonal + pair_sum
    return (weights, MASS_SHIFT + diagonal)


def stencil_apply(padded, weights, diagonal):
    result = diagonal * padded[1:-1, 1:-1]
    for position, offset in enumerate(HALF_STEPS):
        forward_weight, backward_weight = weights[position]
        result = result - forward_weight * neighbour(padded, offset[0], offset[1], offset[2])
        result = result - backward_weight * neighbour(padded, -offset[0], -offset[1], -offset[2])
    return result


def coarse_panels(weights, diagonal, own_onehot, halo_onehot):
    stencil_terms = [((0, 0, 0), diagonal)]
    for position, offset in enumerate(HALF_STEPS):
        forward_weight, backward_weight = weights[position]
        stencil_terms.append((offset, -forward_weight))
        stencil_terms.append(((-offset[0], -offset[1], -offset[2]), -backward_weight))
    reached = None
    for offset, entry_value in stencil_terms:
        portion = shift_radial(own_onehot * entry_value[None], -offset[2])
        placed = jnp.pad(
            portion,
            ((0, 0), (1 + offset[0], 1 - offset[0]), (1 + offset[1], 1 - offset[1]), (0, 0)),
        )
        reached = placed if reached is None else reached + placed
    rows_axial = own_onehot.shape[1]
    rows_circ = own_onehot.shape[2]
    axial_parts = ((1, rows_axial + 1), (rows_axial + 1, rows_axial + 2))
    circ_parts = ((0, 1), (1, rows_circ + 1), (rows_circ + 1, rows_circ + 2))
    panel_rows = []
    for axial_start, axial_stop in axial_parts:
        panel_line = []
        for circ_start, circ_stop in circ_parts:
            panel_line.append(
                jnp.einsum(
                    "kxyr,lxyr->kl",
                    reached[:, axial_start:axial_stop, circ_start:circ_stop],
                    halo_onehot[:, axial_start:axial_stop, circ_start:circ_stop],
                    precision=PRECISE,
                )
            )
        panel_rows.append(jnp.stack(panel_line))
    return jnp.transpose(jnp.stack(panel_rows), (2, 0, 1, 3))


def cycle_blocks(panels):
    cycle_size = panels.shape[0]
    positions = jnp.arange(cycle_size, dtype=jnp.int32)
    shifts = jnp.stack(
        [
            ((positions[:, None] + offset) % cycle_size == positions[None, :]).astype(jnp.float32)
            for offset in (-1, 0, 1)
        ]
    )
    blocks = jnp.einsum("sjm,jkrsl->rjkml", shifts, panels, precision=PRECISE)
    return blocks.reshape(2, cycle_size * LABELS, cycle_size * LABELS)


def block_factor(diagonal_blocks, upper_blocks):
    block_size = diagonal_blocks.shape[1]
    identity = jnp.eye(block_size, dtype=jnp.float32)

    def advance(carried, inputs):
        inverse_prev, upper_prev = carried
        diagonal_now, upper_now = inputs
        coupling = jnp.dot(inverse_prev, upper_prev, precision=PRECISE)
        schur_block = diagonal_now - jnp.dot(coupling.T, coupling, precision=PRECISE)
        factor_now = jnp.linalg.cholesky(schur_block)
        inverse_now = lax.linalg.triangular_solve(factor_now, identity, left_side=True, lower=True)
        return ((inverse_now, upper_now), (inverse_now, coupling))

    start = (identity, jnp.zeros((block_size, block_size), jnp.float32))
    unused, (inverses, couplings) = lax.scan(advance, start, (diagonal_blocks, upper_blocks))
    return (inverses, couplings)


def coarse_solve(inverses, couplings, coarse_rhs):
    cycle_count, block_size = (inverses.shape[0], inverses.shape[1])
    parts = coarse_rhs.reshape(cycle_count, block_size)

    def forward(previous, members):
        inverse_now, coupling, part_now = members
        target = part_now - jnp.dot(coupling.T, previous, precision=PRECISE)
        solved = jnp.dot(inverse_now, target, precision=PRECISE)
        return (solved, solved)

    unused, middle = lax.scan(
        forward, jnp.zeros((block_size,), jnp.float32), (inverses, couplings, parts)
    )
    couplings_next = jnp.concatenate(
        [couplings[1:], jnp.zeros((1, block_size, block_size), jnp.float32)], axis=0
    )

    def backward(solved_next, members):
        inverse_now, coupling_next, middle_now = members
        target = middle_now - jnp.dot(coupling_next, solved_next, precision=PRECISE)
        solved = jnp.dot(inverse_now.T, target, precision=PRECISE)
        return (solved, solved)

    unused_last, solution_parts = lax.scan(
        backward,
        jnp.zeros((block_size,), jnp.float32),
        (inverses, couplings_next, middle),
        reverse=True,
    )
    return solution_parts.reshape(-1)


def spread_coarse(coarse_values, halo_onehot, axial_index, circ_index, cycle_count, cycle_size):
    by_device = coarse_values.reshape(cycle_count, cycle_size, LABELS)
    grid_rows = []
    for move_axial in (-1, 0, 1):
        target = axial_index + move_axial
        present = jnp.logical_and(target >= 0, target < cycle_count)
        cycle_row = lax.dynamic_index_in_dim(
            by_device, jnp.clip(target, 0, cycle_count - 1), 0, keepdims=False
        )
        line_values = []
        for move_circ in (-1, 0, 1):
            beside = lax.dynamic_index_in_dim(
                cycle_row, (circ_index + move_circ) % cycle_size, 0, keepdims=False
            )
            line_values.append(jnp.where(present, beside, jnp.zeros_like(beside)))
        grid_rows.append(jnp.stack(line_values))
    regional = jnp.stack(grid_rows)
    rows_axial = halo_onehot.shape[1] - 2
    rows_circ = halo_onehot.shape[2] - 2
    regional = jnp.repeat(
        regional, np.array([1, rows_axial, 1]), axis=0, total_repeat_length=rows_axial + 2
    )
    regional = jnp.repeat(
        regional, np.array([1, rows_circ, 1]), axis=1, total_repeat_length=rows_circ + 2
    )
    return jnp.einsum("lxyr,xyl->xyr", halo_onehot, regional, precision=PRECISE)


def shards(right_side, stiffness, material, groups):
    cycle_count = lax.axis_size(AXIAL)
    cycle_size = lax.axis_size(CIRC)
    axial_index = lax.axis_index(AXIAL)
    circ_index = lax.axis_index(CIRC)
    labels_pad = extend_labels(jnp.stack([material, groups]))
    weights, diagonal = edge_weights(extend_field(stiffness), labels_pad[0])
    own_onehot = class_onehot(groups, LABELS)
    halo_onehot = class_onehot(labels_pad[1], LABELS)
    panels = coarse_panels(weights, diagonal, own_onehot, halo_onehot)
    cycle_panels = collect(panels[None], CIRC, 0)
    own_cycle = cycle_blocks(cycle_panels)
    all_cycles = lax.all_gather(own_cycle[None], AXIAL, axis=0, tiled=True)
    inverses, couplings = block_factor(all_cycles[:, 0], all_cycles[:, 1])

    def project(field):
        return jnp.einsum("kxyr,xyr->k", own_onehot, field, precision=PRECISE)

    def coarse_gather(field, partial_sum):
        gathered = gather_axes(
            jnp.concatenate([project(field), partial_sum[None]])[None], AXIAL_CIRC, (0, 2, 3, 1), 0
        )
        return (gathered[:, :LABELS].reshape(-1), jnp.sum(gathered[:, LABELS]))

    def spread(coarse_rhs):
        return spread_coarse(
            coarse_solve(inverses, couplings, coarse_rhs),
            halo_onehot,
            axial_index,
            circ_index,
            cycle_count,
            cycle_size,
        )

    def deflate(residual_now):
        residual_image = stencil_apply(extend_field(residual_now), weights, diagonal)
        partial_sum = jnp.sum(residual_now * residual_now)
        coarse_rhs, norm_value = coarse_gather(residual_image, partial_sum)
        return (residual_image, norm_value, spread(coarse_rhs))

    start_rhs, unused_norm = coarse_gather(right_side, jnp.zeros((), jnp.float32))
    start_pad = spread(start_rhs)
    solution = start_pad[1:-1, 1:-1]
    residual = right_side - stencil_apply(start_pad, weights, diagonal)
    residual_image, norm_now, spread_pad = deflate(residual)
    direction = residual - spread_pad[1:-1, 1:-1]
    direction_image = None
    direction_image = residual_image - stencil_apply(spread_pad, weights, diagonal)
    for iteration in range(ITERS):
        curvature = over_axes(jnp.sum(direction * direction_image), AXIAL_CIRC)
        step_length = norm_now / curvature
        solution = solution + step_length * direction
        residual = residual - step_length * direction_image
        if iteration + 1 < ITERS:
            residual_image, norm_next, spread_pad = deflate(residual)
            beta_ratio = norm_next / norm_now
            shifted = spread_pad[1:-1, 1:-1]
            direction_image = (
                beta_ratio * direction_image
                + residual_image
                - stencil_apply(spread_pad, weights, diagonal)
            )
            direction = beta_ratio * direction + residual - shifted
            norm_now = norm_next
    return (solution, residual)


def solution(mesh):
    split = Mesh(mesh.devices.reshape(8, 2, 4, 4), ("axial_0", "axial_1", "circ_0", "circ_1"))
    placed = (
        P(AXIAL, CIRC, None),
        P(AXIAL, CIRC, None),
        P(AXIAL, CIRC, None),
        P(AXIAL, CIRC, None),
    )
    return jax.shard_map(
        shards,
        mesh=split,
        in_specs=placed,
        out_specs=(P(AXIAL, CIRC, None), P(AXIAL, CIRC, None)),
        check_vma=False,
    )
```

profile of v0, /device:TPU:10, one launch (start us, length us, event | category | flops | bytes accessed | tf_op | source)
XLA Modules:
  0.0 995.1 jit_solution(13249270050933131890)
XLA Ops:
  69.3 12.1 %all-to-all-start = ((f32[16,1,384]{2,1,0:T(1,128)}), f32[16,1,384]{2,1,0:T(1,128)S(1)}, u32[]{:S(2)}, u32[]{:S(2)}) async-start(f32[16,1,384]{2,1,0:T(1,128)} %reshape.1223), calls=%async_computation | async-start | bytes 49152 | tf_op jit(solution)/shard_map/all_to_all | solution.py:50
  97.4 20.7 %all-reduce.154 = f32[72]{0:T(128)S(1)} all-reduce(f32[72]{0:T(128)S(1)} %maximum_dynamic-update-slice_fusion), channel_id=2, replica_groups=mesh['axial_0'=8,'axial_1'=2,'circ_0'=4,'circ_1'=4] {'axial_0'}, use_global_device_ids=true, to_apply=%add.154 | all-reduce | flops 72 | bytes 576
  145.9 415.9 %while.113 = (s32[]{:T(128)}, f32[128,128]{1,0:T(8,128)S(1)}, f32[128,128]{1,0:T(8,128)S(1)}, f32[16,128,128]{2,1,0:T(8,128)}, f32[16,128,128]{2,1,0:T(8,128)}, ...) while((s32[]{:T(128)}, f32[128,128]{1,0:T(8,128)S(1)}, ...), condition=%wide.region_3.4_spmd.clone, body=%wide.region_0.3_spmd.clone.sunk | while | flops 75694208 | bytes 1575007 | solution.py:235
  148.3 11.7 %cholesky.75 = f32[128,128]{1,0:T(8,128)S(1)} custom-call(f32[128,128]{1,0:T(8,128)S(1)} %fusion.439), custom_call_target="Cholesky" | custom-call | tf_op jit(solution)/shard_map/while/body/eval_jaxpr/jit(cholesky)/cholesky | solution.py:230
  174.2 11.7 %cholesky.75 = f32[128,128]{1,0:T(8,128)S(1)} custom-call(f32[128,128]{1,0:T(8,128)S(1)} %fusion.439), custom_call_target="Cholesky" | custom-call | tf_op jit(solution)/shard_map/while/body/eval_jaxpr/jit(cholesky)/cholesky | solution.py:230
  200.2 11.7 %cholesky.75 = f32[128,128]{1,0:T(8,128)S(1)} custom-call(f32[128,128]{1,0:T(8,128)S(1)} %fusion.439), custom_call_target="Cholesky" | custom-call | tf_op jit(solution)/shard_map/while/body/eval_jaxpr/jit(cholesky)/cholesky | solution.py:230
  226.2 11.7 %cholesky.75 = f32[128,128]{1,0:T(8,128)S(1)} custom-call(f32[128,128]{1,0:T(8,128)S(1)} %fusion.439), custom_call_target="Cholesky" | custom-call | tf_op jit(solution)/shard_map/while/body/eval_jaxpr/jit(cholesky)/cholesky | solution.py:230
  252.2 11.7 %cholesky.75 = f32[128,128]{1,0:T(8,128)S(1)} custom-call(f32[128,128]{1,0:T(8,128)S(1)} %fusion.439), custom_call_target="Cholesky" | custom-call | tf_op jit(solution)/shard_map/while/body/eval_jaxpr/jit(cholesky)/cholesky | solution.py:230
  278.2 11.7 %cholesky.75 = f32[128,128]{1,0:T(8,128)S(1)} custom-call(f32[128,128]{1,0:T(8,128)S(1)} %fusion.439), custom_call_target="Cholesky" | custom-call | tf_op jit(solution)/shard_map/while/body/eval_jaxpr/jit(cholesky)/cholesky | solution.py:230
  304.1 11.7 %cholesky.75 = f32[128,128]{1,0:T(8,128)S(1)} custom-call(f32[128,128]{1,0:T(8,128)S(1)} %fusion.439), custom_call_target="Cholesky" | custom-call | tf_op jit(solution)/shard_map/while/body/eval_jaxpr/jit(cholesky)/cholesky | solution.py:230
  330.1 11.7 %cholesky.75 = f32[128,128]{1,0:T(8,128)S(1)} custom-call(f32[128,128]{1,0:T(8,128)S(1)} %fusion.439), custom_call_target="Cholesky" | custom-call | tf_op jit(solution)/shard_map/while/body/eval_jaxpr/jit(cholesky)/cholesky | solution.py:230
  356.1 11.7 %cholesky.75 = f32[128,128]{1,0:T(8,128)S(1)} custom-call(f32[128,128]{1,0:T(8,128)S(1)} %fusion.439), custom_call_target="Cholesky" | custom-call | tf_op jit(solution)/shard_map/while/body/eval_jaxpr/jit(cholesky)/cholesky | solution.py:230
  563.0 33.8 %while.107 = (s32[]{:T(128)}, f32[128]{0:T(128)S(1)}, f32[16,128]{1,0:T(8,128)S(1)}, f32[16,128,128]{2,1,0:T(8,128)}, f32[16,128]{1,0:T(8,128)S(1)}, /*index=5*/f32[16,128,128]{2,1,0:T(8,128)}, s32[]{:T(128)}, s32[]{:T(128)}) while((s32[]{:T(128)}, f32[128]{0:T(128)S(1)}, f32[16,128]{1,0:T(8,128)S(1)}, f32[16,128,128]{2,1,0:T(8,128)}, ...), condition=%wide.region_5.6_spmd, body=%wide.region_4.5_spmd.sunk | while | flops 393346 | bytes 136281 | solution.py:249
  596.9 20.4 %while.108 = (s32[]{:T(128)}, f32[128]{0:T(128)S(1)}, f32[16,128]{1,0:T(8,128)S(1)}, f32[16,128,128]{2,1,0:T(8,128)}, f32[16,128]{1,0:T(8,128)S(1)}, /*index=5*/...) while((s32[]{:T(128)}, f32[128]{0:T(128)S(1)}, f32[16,128]{1,0:T(8,128)S(1)}, ...), condition=%wide.region_7.8_spmd, body=%wide.region_6.7_spmd.sunk | while | flops 393347 | bytes 135793 | solution.py:262
  639.0 18.2 %all-reduce.155 = f32[72]{0:T(128)S(1)} all-reduce(f32[72]{0:T(128)S(1)} %maximum_dynamic-update-slice_fusion.1), channel_id=3, replica_groups=mesh['axial_0'=8,'axial_1'=2,'circ_0'=4,'circ_1'=4] {'axial_0'}, use_global_device_ids=true, to_apply=%add.155 | all-reduce | flops 72 | bytes 576
  668.7 13.1 %all_gather.46 = f32[128,1,9]{2,0,1:T(8,128)S(1)} all-gather(f32[32,1,9]{2,0,1:T(8,128)S(1)} %all_gather.45), channel_id=1, replica_groups=mesh['axial_0'=8,'axial_1'=2,'circ_0'=4,'circ_1'=4] {'circ_1'}, dimensions={0}, use_global_device_ids=true | all-gather | bytes 5760 | tf_op jit(solution)/shard_map/all_gather | solution.py:67
  683.9 33.7 %while.109 = (s32[]{:T(128)}, f32[128]{0:T(128)S(1)}, f32[16,128]{1,0:T(8,128)S(1)}, f32[16,128,128]{2,1,0:T(8,128)}, f32[16,128]{1,0:T(8,128)S(1)}, /*index=5*/f32[16,128,128]{2,1,0:T(8,128)}, s32[]{:T(128)}, s32[]{:T(128)}) while((s32[]{:T(128)}, f32[128]{0:T(128)S(1)}, f32[16,128]{1,0:T(8,128)S(1)}, f32[16,128,128]{2,1,0:T(8,128)}, ...), condition=%wide.region_17.20_spmd, body=%wide.region_16.19_spmd.sunk | while | flops 393346 | bytes 136281 | solution.py:249
  717.7 33.8 %while.110 = (s32[]{:T(128)}, f32[128]{0:T(128)S(1)}, f32[16,128]{1,0:T(8,128)S(1)}, f32[16,128,128]{2,1,0:T(8,128)}, f32[16,128]{1,0:T(8,128)S(1)}, /*index=5*/...) while((s32[]{:T(128)}, f32[128]{0:T(128)S(1)}, f32[16,128]{1,0:T(8,128)S(1)}, ...), condition=%wide.region_19.22_spmd, body=%wide.region_18.21_spmd.sunk | while | flops 393347 | bytes 135793 | solution.py:262
  758.6 16.6 %psum.56 = f32[]{:T(128)} all-reduce(f32[]{:T(128)} %get-tuple-element.743), channel_id=1, replica_groups=mesh['axial_0'=8,'axial_1'=2,'circ_0'=4,'circ_1'=4] {'axial_0'}, use_global_device_ids=true, to_apply=%region_27.30 | all-reduce | flops 1 | bytes 8 | tf_op jit(solution)/shard_map/psum | solution.py:79
  818.5 16.5 %all-reduce.156 = f32[72]{0:T(128)S(1)} all-reduce(f32[72]{0:T(128)S(1)} %maximum_dynamic-update-slice_fusion.2), channel_id=4, replica_groups=mesh['axial_0'=8,'axial_1'=2,'circ_0'=4,'circ_1'=4] {'axial_0'}, use_global_device_ids=true, to_apply=%add.156 | all-reduce | flops 72 | bytes 576
  845.9 13.9 %all_gather.50 = f32[128,1,9]{2,0,1:T(8,128)S(1)} all-gather(f32[32,1,9]{2,0,1:T(8,128)S(1)} %all_gather.49), channel_id=1, replica_groups=mesh['axial_0'=8,'axial_1'=2,'circ_0'=4,'circ_1'=4] {'circ_1'}, dimensions={0}, use_global_device_ids=true | all-gather | bytes 5760 | tf_op jit(solution)/shard_map/all_gather | solution.py:67
  862.9 33.8 %while.111 = (s32[]{:T(128)}, f32[128]{0:T(128)S(1)}, f32[16,128]{1,0:T(8,128)S(1)}, f32[16,128,128]{2,1,0:T(8,128)}, f32[16,128]{1,0:T(8,128)S(1)}, /*index=5*/f32[16,128,128]{2,1,0:T(8,128)}, s32[]{:T(128)}, s32[]{:T(128)}) while((s32[]{:T(128)}, f32[128]{0:T(128)S(1)}, f32[16,128]{1,0:T(8,128)S(1)}, f32[16,128,128]{2,1,0:T(8,128)}, ...), condition=%wide.region_34.37_spmd, body=%wide.region_33.36_spmd.sunk | while | flops 393346 | bytes 136281 | solution.py:249
  896.7 33.8 %while.112 = (s32[]{:T(128)}, f32[128]{0:T(128)S(1)}, f32[16,128]{1,0:T(8,128)S(1)}, f32[16,128,128]{2,1,0:T(8,128)}, f32[16,128]{1,0:T(8,128)S(1)}, /*index=5*/...) while((s32[]{:T(128)}, f32[128]{0:T(128)S(1)}, f32[16,128]{1,0:T(8,128)S(1)}, ...), condition=%wide.region_36.39_spmd, body=%wide.region_35.38_spmd.sunk | while | flops 393347 | bytes 135793 | solution.py:262
  941.5 17.5 %psum.60 = f32[]{:T(128)} all-reduce(f32[]{:T(128)} %get-tuple-element.739), channel_id=1, replica_groups=mesh['axial_0'=8,'axial_1'=2,'circ_0'=4,'circ_1'=4] {'axial_0'}, use_global_device_ids=true, to_apply=%region_44.47 | all-reduce | flops 1 | bytes 8 | tf_op jit(solution)/shard_map/psum | solution.py:79
  (875 shorter events, 736.4 us)
Async XLA Ops:
  7.2 23.1 %copy-start.48 = (s32[8,16,256]{2,1,0:T(8,128)S(1)}, s32[8,16,256]{2,1,0:T(8,128)}, u32[]{:S(2)}) copy-start(s32[8,16,256]{2,1,0:T(8,128)} %param.43) | copy-start | bytes 393220
  7.2 23.1 %copy-start.47 = (s32[8,16,256]{2,1,0:T(8,128)S(1)}, s32[8,16,256]{2,1,0:T(8,128)}, u32[]{:S(2)}) copy-start(s32[8,16,256]{2,1,0:T(8,128)} %param.44) | copy-start | bytes 393220
  8.2 11.6 %collective-permute-start = (s32[2,8,1,256]{3,2,1,0:T(1,128)S(1)}, s32[2,8,1,256]{3,2,1,0:T(1,128)S(1)}, u32[]{:S(2)}, u32[]{:S(2)}) collective-permute-start(s32[2,8,1,256]{3,2,1,0:T(1,128)S(1)} %get-tuple-element.828), channel_id=1, source_target_pairs={{0,1},{1,2},{2,3},{3,4},{4,5},{5,6},{6,7},{7,8},{8,9},{9,10},{10,1... | collective-permute-start | bytes 49160 | tf_op jit(solution)/shard_map/ppermute | solution.py:42
  9.9 10.0 %collective-permute-start.1 = (s32[2,8,1,256]{3,2,1,0:T(1,128)S(1)}, s32[2,8,1,256]{3,2,1,0:T(1,128)S(1)}, u32[]{:S(2)}, u32[]{:S(2)}) collective-permute-start(s32[2,8,1,256]{3,2,1,0:T(1,128)S(1)} %get-tuple-element.829), channel_id=1, source_target_pairs={{1,0},{2,1},{3,2},{4,3},{5,4},{6,5},{7,6},{8,7},{9,8},{10,9},{11,1... | collective-permute-start | bytes 49160 | tf_op jit(solution)/shard_map/ppermute | solution.py:43
  11.2 4.3 collective-permute-start.4
  12.9 3.7 collective-permute-start.5
  15.1 32.0 %copy-start.44 = (pred[8,8,16,256]{3,0,1,2:T(8,128)(4,1)}, pred[8,8,16,256]{3,0,1,2:T(8,128)(4,1)S(1)}, u32[]{:S(2)}) copy-start(pred[8,8,16,256]{3,0,1,2:T(8,128)(4,1)S(1)} %iota_compare_fusion.6) | copy-start | bytes 786436
  17.3 10.4 %collective-permute-start.6 = (f32[1,18,256]{2,1,0:T(8,128)S(1)}, f32[1,18,256]{2,1,0:T(8,128)S(1)}, u32[]{:S(2)}, u32[]{:S(2)}) collective-permute-start(f32[1,18,256]{2,1,0:T(8,128)S(1)} %get-tuple-element.934), channel_id=1, source_target_pairs={{0,16},{16,32},{32,48},{48,64},{64,80},{80,96},{96,112},{112,128},... | collective-permute-start | bytes 55304 | tf_op jit(solution)/shard_map/ppermute | solution.py:42
  18.6 9.1 collective-permute-start.7
  20.7 7.1 collective-permute-start.2
  25.9 4.4 collective-permute-start.3
  69.3 17.5 %all-to-all-start = ((f32[16,1,384]{2,1,0:T(1,128)}), f32[16,1,384]{2,1,0:T(1,128)S(1)}, u32[]{:S(2)}, u32[]{:S(2)}) async-start(f32[16,1,384]{2,1,0:T(1,128)} %reshape.1223), calls=%async_computation | async-start | bytes 49152 | tf_op jit(solution)/shard_map/all_to_all | solution.py:50
  81.4 61.7 %all-gather.5.cloned.1.call-start = ((), (), s32[]{:S(2)}) async-start(), calls=%async_computation.1 | async-start | bytes 2228224 | tf_op jit(solution)/shard_map/all_gather | solution.py:311
  93.7 49.4 %copy-start.58 = (s32[10]{0:T(128)S(1)}, s32[10]{0:T(128)}, u32[]{:S(2)}) copy-start(s32[10]{0:T(128)} %constant.1462) | copy-start | bytes 124
  93.7 49.4 %copy-start.57 = (s32[18]{0:T(128)S(1)}, s32[18]{0:T(128)}, u32[]{:S(2)}) copy-start(s32[18]{0:T(128)} %constant.1463) | copy-start | bytes 220
  623.2 3.7 collective-permute-start.8
  625.3 4.3 collective-permute-start.9
  629.7 4.7 collective-permute-start.10
  631.0 3.9 collective-permute-start.11
  683.8 68.2 %copy-start.49 = (f32[2,4,4,8,1,9]{5,1,2,0,3,4:T(4,128)}, f32[2,4,4,8,1,9]{5,1,2,0,3,4:T(4,128)S(1)}, u32[]{:S(2)}) copy-start(f32[2,4,4,8,1,9]{5,1,2,0,3,4:T(4,128)S(1)} %copy.274) | copy-start | bytes 27652
  805.3 3.7 collective-permute-start.12
  805.4 3.7 collective-permute-start.13
  809.1 4.5 collective-permute-start.14
  810.4 3.9 collective-permute-start.15
  (54 other events, 131.2 us)
Sparse Core Ops, SparseCore 0:
  93.8 43.4 all-gather.4
where the time goes:
time: 1010 us; the launch traced here: 995 us
  other arithmetic  409 us (40%)
  matrix products  235 us (23%)
  blocking collectives  218 us (22%)
  local copies, waits for them, and re-layouts  51.7 us (5%)
  starting transfers between devices  39.7 us (4%)
  between operations  21.3 us (2%)
  waiting for transfers between devices  16 us (2%)
    another operation x48, other arithmetic, advance(): factor_now = jnp.linalg.cholesky(schur_block)  198 us
    another operation x32, other arithmetic, advance(): lax.linalg.triangular_solve(factor_now, identity, left_side=True, lower=T...  167 us
    psum x8, blocking collectives, over_axes(): return functools.reduce(lax.psum, axes, array)  85.2 us
    all_gather x9, blocking collectives, gather_in_order(): parts = lax.all_gather(parts, axes[k], axis=0, tiled=True)  77.8 us
    unnamed x3, blocking collectives  55.5 us
    dot_general x48, matrix products, backward(): solved = jnp.dot(inverse_now.T, target, precision=PRECISE)  49.9 us
    dot_general x48, matrix products, forward(): solved = jnp.dot(inverse_now, target, precision=PRECISE)  49.3 us
    dot_general x48, matrix products, forward(): target = part_now - jnp.dot(coupling.T, previous, precision=PRECISE)  48.1 us
  transfers between devices with their start and end apart: 18, of which 10 were waited for; matrix products, arithmetic and copies ran while one was open for 1% of the time, Pallas kernels for 0%

commit v1 on v0

--- a/solution.py
+++ b/solution.py
@@ -64,7 +64,10 @@
 def gather_in_order(array, axes, turns):
     parts = array[None]
     for k in turns:
-        parts = lax.all_gather(parts, axes[k], axis=0, tiled=True)
+        piece_in = axes[k]
+        r_now = jnp.stack([parts for _ in range(lax.axis_size(piece_in))], 0)
+        y = lax.all_to_all(r_now, piece_in, 0, 0)
+        parts = jnp.concatenate(y, 0)
     held = [lax.axis_size(axes[k]) for k in reversed(turns)]
     parts = parts.reshape(*held, *array.shape)
     turned = sorted(range(len(turns)), key=lambda place: turns[len(turns) - 1 - place])

time: 1010 us -> 993 us (0.983)
  blocking collectives: 218 us -> 131 us
  starting transfers between devices: 39.7 us -> 76.6 us
  waiting for transfers between devices: 16 us -> 39 us
    all_gather x9 -> x0, blocking collectives: 77.8 us -> none  [gather_in_order(): parts = lax.all_gather(parts, axes[k], axis=0, tiled=True)]
    unnamed x3 -> x0, blocking collectives: 55.5 us -> none
    all_to_all x0 -> x7, blocking collectives: none -> 55.2 us  [gather_in_order(): y = lax.all_to_all(r_now, piece_in, 0, 0)]
    all_to_all x0 -> x5, starting transfers between devices: none -> 36.9 us  [gather_in_order(): y = lax.all_to_all(r_now, piece_in, 0, 0)]
    all_to_all x0 -> x5, waiting for transfers between devices: none -> 23.1 us  [gather_in_order(): y = lax.all_to_all(r_now, piece_in, 0, 0)]
  transfers between devices with their start and end apart: 18 -> 23, of which waited for: 10 -> 15; matrix products, arithmetic and copies ran while one was open for 1% -> 1% of each run, Pallas kernels for 0% -> 0%
where the time goes in v1:
time: 993 us; the launch traced here: 978 us
  other arithmetic  414 us (42%)
  matrix products  235 us (24%)
  blocking collectives  131 us (13%)
  starting transfers between devices  76.6 us (8%)
  local copies, waits for them, and re-layouts  58.6 us (6%)
  waiting for transfers between devices  39 us (4%)
  between operations  20.6 us (2%)
    another operation x48, other arithmetic, advance(): factor_now = jnp.linalg.cholesky(schur_block)  198 us
    another operation x32, other arithmetic, advance(): lax.linalg.triangular_solve(factor_now, identity, left_side=True, lower=T...  167 us
    psum x8, blocking collectives, over_axes(): return functools.reduce(lax.psum, axes, array)  76.1 us
    all_to_all x7, blocking collectives, gather_in_order(): y = lax.all_to_all(r_now, piece_in, 0, 0)  55.2 us
    dot_general x48, matrix products, backward(): solved = jnp.dot(inverse_now.T, target, precision=PRECISE)  49.9 us
    dot_general x48, matrix products, forward(): solved = jnp.dot(inverse_now, target, precision=PRECISE)  49.3 us
    dot_general x48, matrix products, forward(): target = part_now - jnp.dot(coupling.T, previous, precision=PRECISE)  48.1 us
    all_to_all x5, starting transfers between devices, gather_in_order(): y = lax.all_to_all(r_now, piece_in, 0, 0)  36.9 us
  transfers between devices with their start and end apart: 23, of which 15 were waited for; matrix products, arithmetic and copies ran while one was open for 1% of the time, Pallas kernels for 0%

profile of v1, /device:TPU:10, one launch (start us, length us, event | category | flops | bytes accessed | tf_op | source)
XLA Modules:
  0.0 978.2 jit_solution(3313607496544461670)
XLA Ops:
  69.3 12.1 %all-to-all-start = ((f32[16,1,384]{2,1,0:T(1,128)}), f32[16,1,384]{2,1,0:T(1,128)S(1)}, u32[]{:S(2)}, u32[]{:S(2)}) async-start(f32[16,1,384]{2,1,0:T(1,128)} %reshape.1223), calls=%async_computation | async-start | bytes 49152 | tf_op jit(solution)/shard_map/all_to_all | solution.py:50
  143.1 415.6 %while.113 = (s32[]{:T(128)}, f32[128,128]{1,0:T(8,128)S(1)}, f32[128,128]{1,0:T(8,128)S(1)}, f32[16,128,128]{2,1,0:T(8,128)}, f32[16,128,128]{2,1,0:T(8,128)}, ...) while((s32[]{:T(128)}, f32[128,128]{1,0:T(8,128)S(1)}, ...), condition=%wide.region_3.4_spmd.clone, body=%wide.region_0.3_spmd.clone.sunk | while | flops 75694208 | bytes 1575007 | solution.py:238
  145.5 11.7 %cholesky.75 = f32[128,128]{1,0:T(8,128)S(1)} custom-call(f32[128,128]{1,0:T(8,128)S(1)} %fusion.439), custom_call_target="Cholesky" | custom-call | tf_op jit(solution)/shard_map/while/body/eval_jaxpr/jit(cholesky)/cholesky | solution.py:233
  171.5 11.7 %cholesky.75 = f32[128,128]{1,0:T(8,128)S(1)} custom-call(f32[128,128]{1,0:T(8,128)S(1)} %fusion.439), custom_call_target="Cholesky" | custom-call | tf_op jit(solution)/shard_map/while/body/eval_jaxpr/jit(cholesky)/cholesky | solution.py:233
  197.4 11.7 %cholesky.75 = f32[128,128]{1,0:T(8,128)S(1)} custom-call(f32[128,128]{1,0:T(8,128)S(1)} %fusion.439), custom_call_target="Cholesky" | custom-call | tf_op jit(solution)/shard_map/while/body/eval_jaxpr/jit(cholesky)/cholesky | solution.py:233
  223.4 11.7 %cholesky.75 = f32[128,128]{1,0:T(8,128)S(1)} custom-call(f32[128,128]{1,0:T(8,128)S(1)} %fusion.439), custom_call_target="Cholesky" | custom-call | tf_op jit(solution)/shard_map/while/body/eval_jaxpr/jit(cholesky)/cholesky | solution.py:233
  249.4 11.7 %cholesky.75 = f32[128,128]{1,0:T(8,128)S(1)} custom-call(f32[128,128]{1,0:T(8,128)S(1)} %fusion.439), custom_call_target="Cholesky" | custom-call | tf_op jit(solution)/shard_map/while/body/eval_jaxpr/jit(cholesky)/cholesky | solution.py:233
  275.3 11.7 %cholesky.75 = f32[128,128]{1,0:T(8,128)S(1)} custom-call(f32[128,128]{1,0:T(8,128)S(1)} %fusion.439), custom_call_target="Cholesky" | custom-call | tf_op jit(solution)/shard_map/while/body/eval_jaxpr/jit(cholesky)/cholesky | solution.py:233
  301.3 11.7 %cholesky.75 = f32[128,128]{1,0:T(8,128)S(1)} custom-call(f32[128,128]{1,0:T(8,128)S(1)} %fusion.439), custom_call_target="Cholesky" | custom-call | tf_op jit(solution)/shard_map/while/body/eval_jaxpr/jit(cholesky)/cholesky | solution.py:233
  327.3 11.7 %cholesky.75 = f32[128,128]{1,0:T(8,128)S(1)} custom-call(f32[128,128]{1,0:T(8,128)S(1)} %fusion.439), custom_call_target="Cholesky" | custom-call | tf_op jit(solution)/shard_map/while/body/eval_jaxpr/jit(cholesky)/cholesky | solution.py:233
  353.2 11.7 %cholesky.75 = f32[128,128]{1,0:T(8,128)S(1)} custom-call(f32[128,128]{1,0:T(8,128)S(1)} %fusion.439), custom_call_target="Cholesky" | custom-call | tf_op jit(solution)/shard_map/while/body/eval_jaxpr/jit(cholesky)/cholesky | solution.py:233
  379.2 11.7 %cholesky.75 = f32[128,128]{1,0:T(8,128)S(1)} custom-call(f32[128,128]{1,0:T(8,128)S(1)} %fusion.439), custom_call_target="Cholesky" | custom-call | tf_op jit(solution)/shard_map/while/body/eval_jaxpr/jit(cholesky)/cholesky | solution.py:233
  405.1 11.7 %cholesky.75 = f32[128,128]{1,0:T(8,128)S(1)} custom-call(f32[128,128]{1,0:T(8,128)S(1)} %fusion.439), custom_call_target="Cholesky" | custom-call | tf_op jit(solution)/shard_map/while/body/eval_jaxpr/jit(cholesky)/cholesky | solution.py:233
  431.1 11.7 %cholesky.75 = f32[128,128]{1,0:T(8,128)S(1)} custom-call(f32[128,128]{1,0:T(8,128)S(1)} %fusion.439), custom_call_target="Cholesky" | custom-call | tf_op jit(solution)/shard_map/while/body/eval_jaxpr/jit(cholesky)/cholesky | solution.py:233
  560.0 33.8 %while.107 = (s32[]{:T(128)}, f32[128]{0:T(128)S(1)}, f32[16,128]{1,0:T(8,128)S(1)}, f32[16,128,128]{2,1,0:T(8,128)}, f32[16,128]{1,0:T(8,128)S(1)}, /*index=5*/f32[16,128,128]{2,1,0:T(8,128)}, s32[]{:T(128)}, s32[]{:T(128)}) while((s32[]{:T(128)}, f32[128]{0:T(128)S(1)}, f32[16,128]{1,0:T(8,128)S(1)}, f32[16,128,128]{2,1,0:T(8,128)}, ...), condition=%wide.region_5.6_spmd, body=%wide.region_4.5_spmd.sunk | while | flops 393346 | bytes 136281 | solution.py:252
  593.9 20.4 %while.108 = (s32[]{:T(128)}, f32[128]{0:T(128)S(1)}, f32[16,128]{1,0:T(8,128)S(1)}, f32[16,128,128]{2,1,0:T(8,128)}, f32[16,128]{1,0:T(8,128)S(1)}, /*index=5*/...) while((s32[]{:T(128)}, f32[128]{0:T(128)S(1)}, f32[16,128]{1,0:T(8,128)S(1)}, ...), condition=%wide.region_7.8_spmd, body=%wide.region_6.7_spmd.sunk | while | flops 393347 | bytes 135793 | solution.py:265
  634.4 13.8 %all_to_all.66 = f32[8,1,1,9]{3,2,1,0:T(1,128)S(1)} all-to-all(f32[8,1,1,9]{3,2,1,0:T(1,128)S(1)} %stack.204), channel_id=1, replica_groups=mesh['axial_0'=8,'axial_1'=2,'circ_0'=4,'circ_1'=4] {'axial_0'}, dimensions={0} | all-to-all | bytes 576 | tf_op jit(solution)/shard_map/all_to_all | solution.py:69
  676.6 33.7 %while.109 = (s32[]{:T(128)}, f32[128]{0:T(128)S(1)}, f32[16,128]{1,0:T(8,128)S(1)}, f32[16,128,128]{2,1,0:T(8,128)}, f32[16,128]{1,0:T(8,128)S(1)}, /*index=5*/f32[16,128,128]{2,1,0:T(8,128)}, s32[]{:T(128)}, s32[]{:T(128)}) while((s32[]{:T(128)}, f32[128]{0:T(128)S(1)}, f32[16,128]{1,0:T(8,128)S(1)}, f32[16,128,128]{2,1,0:T(8,128)}, ...), condition=%wide.region_17.20_spmd, body=%wide.region_16.19_spmd.sunk | while | flops 393346 | bytes 136281 | solution.py:252
  710.4 33.8 %while.110 = (s32[]{:T(128)}, f32[128]{0:T(128)S(1)}, f32[16,128]{1,0:T(8,128)S(1)}, f32[16,128,128]{2,1,0:T(8,128)}, f32[16,128]{1,0:T(8,128)S(1)}, /*index=5*/...) while((s32[]{:T(128)}, f32[128]{0:T(128)S(1)}, f32[16,128]{1,0:T(8,128)S(1)}, ...), condition=%wide.region_19.22_spmd, body=%wide.region_18.21_spmd.sunk | while | flops 393347 | bytes 135793 | solution.py:265
  751.3 15.4 %psum.56 = f32[]{:T(128)} all-reduce(f32[]{:T(128)} %get-tuple-element.757), channel_id=1, replica_groups=mesh['axial_0'=8,'axial_1'=2,'circ_0'=4,'circ_1'=4] {'axial_0'}, use_global_device_ids=true, to_apply=%region_27.30 | all-reduce | flops 1 | bytes 8 | tf_op jit(solution)/shard_map/psum | solution.py:82
  808.4 14.6 %all_to_all.69 = f32[8,1,1,9]{3,2,1,0:T(1,128)S(1)} all-to-all(f32[8,1,1,9]{3,2,1,0:T(1,128)S(1)} %stack.215), channel_id=1, replica_groups=mesh['axial_0'=8,'axial_1'=2,'circ_0'=4,'circ_1'=4] {'axial_0'}, dimensions={0} | all-to-all | bytes 576 | tf_op jit(solution)/shard_map/all_to_all | solution.py:69
  851.2 33.8 %while.111 = (s32[]{:T(128)}, f32[128]{0:T(128)S(1)}, f32[16,128]{1,0:T(8,128)S(1)}, f32[16,128,128]{2,1,0:T(8,128)}, f32[16,128]{1,0:T(8,128)S(1)}, /*index=5*/f32[16,128,128]{2,1,0:T(8,128)}, s32[]{:T(128)}, s32[]{:T(128)}) while((s32[]{:T(128)}, f32[128]{0:T(128)S(1)}, f32[16,128]{1,0:T(8,128)S(1)}, f32[16,128,128]{2,1,0:T(8,128)}, ...), condition=%wide.region_34.37_spmd, body=%wide.region_33.36_spmd.sunk | while | flops 393346 | bytes 136281 | solution.py:252
  885.0 33.8 %while.112 = (s32[]{:T(128)}, f32[128]{0:T(128)S(1)}, f32[16,128]{1,0:T(8,128)S(1)}, f32[16,128,128]{2,1,0:T(8,128)}, f32[16,128]{1,0:T(8,128)S(1)}, /*index=5*/...) while((s32[]{:T(128)}, f32[128]{0:T(128)S(1)}, f32[16,128]{1,0:T(8,128)S(1)}, ...), condition=%wide.region_36.39_spmd, body=%wide.region_35.38_spmd.sunk | while | flops 393347 | bytes 135793 | solution.py:265
  929.8 15.3 %psum.60 = f32[]{:T(128)} all-reduce(f32[]{:T(128)} %get-tuple-element.753), channel_id=1, replica_groups=mesh['axial_0'=8,'axial_1'=2,'circ_0'=4,'circ_1'=4] {'axial_0'}, use_global_device_ids=true, to_apply=%region_44.47 | all-reduce | flops 1 | bytes 8 | tf_op jit(solution)/shard_map/psum | solution.py:82
  (905 shorter events, 742.6 us)
Async XLA Ops:
  8.2 11.6 %collective-permute-start = (s32[2,8,1,256]{3,2,1,0:T(1,128)S(1)}, s32[2,8,1,256]{3,2,1,0:T(1,128)S(1)}, u32[]{:S(2)}, u32[]{:S(2)}) collective-permute-start(s32[2,8,1,256]{3,2,1,0:T(1,128)S(1)} %get-tuple-element.842), channel_id=1, source_target_pairs={{0,1},{1,2},{2,3},{3,4},{4,5},{5,6},{6,7},{7,8},{8,9},{9,10},{10,1... | collective-permute-start | bytes 49160 | tf_op jit(solution)/shard_map/ppermute | solution.py:42
  9.9 10.0 %collective-permute-start.1 = (s32[2,8,1,256]{3,2,1,0:T(1,128)S(1)}, s32[2,8,1,256]{3,2,1,0:T(1,128)S(1)}, u32[]{:S(2)}, u32[]{:S(2)}) collective-permute-start(s32[2,8,1,256]{3,2,1,0:T(1,128)S(1)} %get-tuple-element.843), channel_id=1, source_target_pairs={{1,0},{2,1},{3,2},{4,3},{5,4},{6,5},{7,6},{8,7},{9,8},{10,9},{11,1... | collective-permute-start | bytes 49160 | tf_op jit(solution)/shard_map/ppermute | solution.py:43
  11.2 4.3 collective-permute-start.4
  12.9 3.7 collective-permute-start.5
  17.3 10.4 %collective-permute-start.6 = (f32[1,18,256]{2,1,0:T(8,128)S(1)}, f32[1,18,256]{2,1,0:T(8,128)S(1)}, u32[]{:S(2)}, u32[]{:S(2)}) collective-permute-start(f32[1,18,256]{2,1,0:T(8,128)S(1)} %get-tuple-element.948), channel_id=1, source_target_pairs={{0,16},{16,32},{32,48},{48,64},{64,80},{80,96},{96,112},{112,128},... | collective-permute-start | bytes 55304 | tf_op jit(solution)/shard_map/ppermute | solution.py:42
  18.6 9.1 collective-permute-start.7
  20.7 7.1 collective-permute-start.2
  25.9 4.4 collective-permute-start.3
  69.3 17.5 %all-to-all-start = ((f32[16,1,384]{2,1,0:T(1,128)}), f32[16,1,384]{2,1,0:T(1,128)S(1)}, u32[]{:S(2)}, u32[]{:S(2)}) async-start(f32[16,1,384]{2,1,0:T(1,128)} %reshape.1223), calls=%async_computation | async-start | bytes 49152 | tf_op jit(solution)/shard_map/all_to_all | solution.py:50
  81.4 59.0 %all-gather.2.cloned.1.call-start = ((), (), s32[]{:S(2)}) async-start(), calls=%async_computation.13 | async-start | bytes 2228224 | tf_op jit(solution)/shard_map/all_gather | solution.py:314
  96.6 19.4 %all-to-all-start.1 = ((f32[8,1,1,9]{3,2,1,0:T(1,128)}), f32[8,1,1,9]{3,2,1,0:T(1,128)S(1)}, u32[]{:S(2)}, u32[]{:S(2)}) async-start(f32[8,1,1,9]{3,2,1,0:T(1,128)} %stack.193), calls=%async_computation.1 | async-start | bytes 8192 | tf_op jit(solution)/shard_map/all_to_all | solution.py:69
  116.6 8.6 all-to-all-start.2
  126.6 8.5 all-to-all-start.3
  620.5 3.7 collective-permute-start.8
  622.0 3.7 collective-permute-start.9
  625.7 4.7 collective-permute-start.10
  627.0 3.9 collective-permute-start.11
  657.7 12.1 %all-to-all-start.7 = ((f32[4,1,288]{2,1,0:T(1,128)}), f32[4,1,288]{2,1,0:T(1,128)S(1)}, u32[]{:S(2)}, u32[]{:S(2)}) async-start(f32[4,1,288]{2,1,0:T(1,128)} %reshape.1227), calls=%async_computation.7 | async-start | bytes 12288 | tf_op jit(solution)/shard_map/all_to_all | solution.py:69
  676.5 68.2 %copy-start.45 = (f32[8,2,4,4,1,9]{5,3,2,1,0,4:T(4,128)}, f32[8,2,4,4,1,9]{5,3,2,1,0,4:T(4,128)S(1)}, u32[]{:S(2)}) copy-start(f32[8,2,4,4,1,9]{5,3,2,1,0,4:T(4,128)S(1)} %copy.445) | copy-start | bytes 27652
  794.1 3.7 collective-permute-start.12
  795.3 3.7 collective-permute-start.13
  799.0 4.5 collective-permute-start.14
  800.3 3.9 collective-permute-start.15
  831.8 11.5 %all-to-all-start.11 = ((f32[4,1,288]{2,1,0:T(1,128)}), f32[4,1,288]{2,1,0:T(1,128)S(1)}, u32[]{:S(2)}, u32[]{:S(2)}) async-start(f32[4,1,288]{2,1,0:T(1,128)} %reshape.1229), calls=%async_computation.11 | async-start | bytes 12288 | tf_op jit(solution)/shard_map/all_to_all | solution.py:69
  (54 other events, 236.0 us)
Sparse Core Ops, SparseCore 0:
  93.8 43.6 all-gather.1
